TPU v7x, 32 devices: a whole 2x2x4 slice. The times are simulated.
32 devices in a mesh: grp: 2 (over x), row: 16 (over z, y, core).
Axes of the slice: x: 2, y: 2, z: 4, core: 2. Of those that a mesh axis runs over, the one named last changes fastest.
Arguments:
- pair_map: bfloat16 [256, 128, 128], P(('grp', 'row')), parts along dimension 0, may hold values from -6 to 6
- norm_gain: float32 [128], replicated, may hold values from 0.1 to 1.9
- w_query: bfloat16 [128, 128], replicated, may hold values from -30 to 30
- w_key: bfloat16 [128, 128], replicated, may hold values from -1 to 1
- w_value: bfloat16 [128, 128], replicated, may hold values from -0.5 to 0.5
- w_gate: bfloat16 [128, 128], replicated, may hold values from -0.5 to 0.5
- w_bias: bfloat16 [128, 4], replicated, may hold values from -12 to 12
- w_output: bfloat16 [128, 128], replicated, may hold values from -0.5 to 0.5
- window_start: int32 [256], P(('grp', 'row')), parts along dimension 0, may hold values from 0 to 63
- key_length: int32 [256], P(('grp', 'row')), parts along dimension 0, may hold values from 32 to 64
Outputs:
- update: bfloat16 [256, 128, 128], P('grp', 'row'), parts along dimension 0
There are 2 independent parts, one for each index of `grp`. A program takes and returns all parts, laid end to end along the dimension named above; an argument that names none is the same for every part. Nothing has to cross between parts.
All inputs are finite; a program needn't handle non-finite values.
Results may differ from a plain program's by a relative error of at most 0.0025.
The roundings to bfloat16 on the way count: a program that leaves them out, or rounds other values in their place, can miss the bound.
Values may be sent and summed in bfloat16 or wider, within the bound.
A program may use at most 128 MiB of HBM per device.

v0:
```python
import math
import jax
import jax.numpy as jnp
from jax import lax
from jax.sharding import PartitionSpec as P

H = 4


def normalize(rows, norm_gain):
    values = rows.astype(jnp.float32)
    center = jnp.mean(values, axis=-1, keepdims=True)
    spread = jnp.mean((values - center) ** 2, axis=-1, keepdims=True)
    return ((values - center) * lax.rsqrt(spread + 1e-05) * norm_gain).astype(jnp.bfloat16)


def local(
    pair_map, norm_gain, w_query, w_key, w_value, w_gate, w_bias, w_output, window_start, key_length
):
    rows, width, channels = pair_map.shape
    head_size = channels // H
    normed = normalize(pair_map, norm_gain)
    stacked = jnp.concatenate([w_query, w_key, w_value, w_gate], axis=1)
    projected = jnp.dot(
        normed.reshape(rows * width, channels), stacked, preferred_element_type=jnp.float32
    )
    query = projected[:, :channels].astype(jnp.bfloat16).reshape(rows, width, H, head_size)
    key = (
        projected[:, channels : 2 * channels]
        .astype(jnp.bfloat16)
        .reshape(rows, width, H, head_size)
    )
    value = (
        projected[:, 2 * channels : 3 * channels]
        .astype(jnp.bfloat16)
        .reshape(rows, width, H, head_size)
    )
    gate = projected[:, 3 * channels :].astype(jnp.bfloat16).reshape(rows, width, channels)
    local_bias = jnp.einsum("rnc,ch->hrn", normed, w_bias, preferred_element_type=jnp.float32)
    positions = jnp.arange(width, dtype=jnp.int32)
    valid = (positions[None, :] >= window_start[:, None]) & (
        positions[None, :] < (window_start + key_length)[:, None]
    )
    factor = 1.0 / head_size**0.5
    all_bias = lax.all_gather(local_bias, "row", axis=1, tiled=True)
    length = all_bias.shape[1]
    block = math.gcd(length, 64)

    def one_block(index):
        offset = index * block
        bias_block = lax.dynamic_slice_in_dim(all_bias, offset, block, 1)
        query_block = lax.dynamic_slice_in_dim(query, offset, block, 1)
        gate_block = lax.dynamic_slice_in_dim(gate, offset, block, 1)
        scores = (
            jnp.einsum("rjhd,rkhd->rhjk", query_block, key, preferred_element_type=jnp.float32)
            * factor
        )
        scores = scores + bias_block[None]
        scores = jnp.where(valid[:, None, None, :], scores, jnp.float32(-1e30))
        top = jnp.max(scores, axis=-1, keepdims=True)
        raised = jnp.exp(scores - top)
        weights = (raised / jnp.sum(raised, axis=-1, keepdims=True)).astype(jnp.bfloat16)
        attended = jnp.einsum("rhjk,rkhd->rjhd", weights, value, preferred_element_type=jnp.float32)
        attended = attended.reshape(rows, block, channels)
        gated = (jax.nn.sigmoid(gate_block.astype(jnp.float32)) * attended).astype(jnp.bfloat16)
        mixed = jnp.dot(
            gated.reshape(rows * block, channels), w_output, preferred_element_type=jnp.float32
        )
        return mixed.astype(jnp.bfloat16).reshape(rows, block, channels)

    blocks = lax.map(one_block, jnp.arange(length // block, dtype=jnp.int32))
    result = jnp.moveaxis(blocks, 0, 1).reshape(rows, length, channels)
    return lax.all_to_all(result, "row", split_axis=1, concat_axis=0, tiled=True)


def solution(mesh):
    return jax.shard_map(
        local,
        mesh=mesh,
        in_specs=(
            P(("grp", "row"), None, None),
            P(),
            P(),
            P(),
            P(),
            P(),
            P(),
            P(),
            P(("grp", "row")),
            P(("grp", "row")),
        ),
        out_specs=P("grp", "row", None),
        check_vma=False,
    )
```

profile of v0, /device:TPU:0, one launch (start us, length us, event | category | flops | bytes accessed | tf_op | source)
XLA Modules:
  0.0 56.8 jit_solution(8926814176208976086)
XLA Ops:
  0.0 1.1 %convert_reduce_fusion = f32[8,128]{1,0:T(8,128)S(1)} fusion(bf16[8,128,128]{2,1,0:T(8,128)(2,1)} %param.12), kind=kLoop, calls=%fused_computation.24 | loop fusion | flops 261120 | bytes 266240 | tf_op jit(solution)/shard_map/reduce_sum | solution.py:12
  1.2 1.3 %fusion.17 = f32[8,128]{1,0:T(8,128)S(1)} fusion(bf16[8,128,128]{2,1,0:T(8,128)(2,1)} %param.12, f32[8,128]{1,0:T(8,128)S(1)} %broadcast_multiply_fusion), kind=kLoop, calls=%fused_computation.27 | loop fusion | flops 523264 | bytes 270336 | tf_op jit(solution)/shard_map/reduce_sum | solution.py:13
  2.5 1.3 %fusion.19 = bf16[8,128,128]{2,1,0:T(8,128)(2,1)S(1)} fusion(bf16[8,128,128]{2,1,0:T(8,128)(2,1)} %param.12, f32[128]{0:T(128)} %param.13, f32[8,128]{1,0:T(8,128)S(1)} %add_rsqrt_fusion, f32[8,128]{1,0:T(8,128)S(1)} %broadcast_multiply_fusion), kind=kLoop, calls=%fused_computation.29 | loop fusion | flops 655360 | bytes 532992 | tf_op jit(solution)/shard_map/convert_element_type | solution.py:14
  3.9 0.4 convolution_convert_fusion.1
  4.3 0.2 fusion.32
  4.5 0.1 copy.37
  4.7 0.1 copy.38
  5.0 0.1 copy.36
  5.2 0.2 convolution_bitcast_fusion
  5.4 23.8 %all_gather.3 = f32[4,128,128]{2,0,1:T(4,128)S(1)} all-gather(f32[4,8,128]{2,0,1:T(4,128)S(1)} %convolution_bitcast_fusion), channel_id=1, replica_groups=mesh['grp'=2,'row'=16] {'row'}, dimensions={1}, use_global_device_ids=true | all-gather | bytes 278528 | tf_op jit(solution)/shard_map/all_gather | solution.py:45
  29.3 13.9 %while.11 = (s32[]{:T(128)}, bf16[2,8,64,128]{3,2,0,1:T(8,128)(2,1)S(1)}, s32[2]{0:T(128)S(1)}, bf16[8,128,128]{2,1,0:T(8,128)(2,1)S(1)}, bf16[8,128,4,32]{1,0,3...) while((s32[]{:T(128)}, ...), condition=%wide.region_5.6_spmd.clone, body=%wide.region_2.5_spmd.clone.sunk | while | flops 70456576 | bytes 6081815 | solution.py:71
  29.3 0.7 %dynamic_slice.27 = s32[1]{0:T(128)} dynamic-slice(s32[2]{0:T(128)S(1)} %get-tuple-element.253, s32[]{:T(128)} %get-tuple-element.236), dynamic_slice_sizes={1} | dynamic-slice | bytes 12 | tf_op jit(solution)/shard_map/while/body/jit(dynamic_index_in_dim)/dynamic_slice | solution.py:71
  30.6 0.1 constant_dynamic-slice_fusion.5
  30.8 0.1 fusion.61
  30.9 0.3 fusion.63
  31.3 0.8 %fusion.62 = f32[8,4,64]{2,1,0:T(4,128)S(1)} fusion(bf16[8,128,4,32]{1,3,2,0:T(8,128)(2,1)S(1)} %get-tuple-element.256, f32[4,64,128]{2,1,0:T(8,128)S(1)} %copy.67, pred[8,128]{1,0:T(8,128)(4,1)S(1)} %fusion.61, bf16[8,64,4,32]{1,0,3,2:T(8,128)(2,1)S(1)} %constant_dynamic-slice_fusion.5), kind=kOutput, calls=%fused_computation.41.clone.1 | convolution fusion | flops 18088064 | bytes 533504 | tf_op jit(solution)/shard_map/while/body/eval_jaxpr/sub | solution.py:61
  32.1 3.6 %fusion.64 = f32[8,4,64,32]{2,3,1,0:T(8,128)S(1)} fusion(bf16[8,128,4,32]{1,3,2,0:T(8,128)(2,1)S(1)} %get-tuple-element.258, f32[8,4,64]{2,1,0:T(4,128)S(1)} %fusion.62, f32[8,4,64,128]{3,2,1,0:T(8,128)S(1)} %fusion.63), kind=kOutput, calls=%fused_computation.9.clone.1 | convolution fusion | flops 17565824 | bytes 1581056 | tf_op jit(solution)/shard_map/while/body/eval_jaxpr/rhjk,rkhd->rjhd/dot_general | solution.py:63
  35.7 0.2 copy.68
  35.9 0.1 multiply_convert_fusion.2
  36.0 0.2 convolution_convert_fusion.3
  36.2 0.7 %dynamic_slice.27 = s32[1]{0:T(128)} dynamic-slice(s32[2]{0:T(128)S(1)} %get-tuple-element.253, s32[]{:T(128)} %get-tuple-element.236), dynamic_slice_sizes={1} | dynamic-slice | bytes 12 | tf_op jit(solution)/shard_map/while/body/jit(dynamic_index_in_dim)/dynamic_slice | solution.py:71
  37.6 0.1 constant_dynamic-slice_fusion.5
  37.8 0.1 fusion.61
  37.9 0.3 fusion.63
  38.2 0.8 %fusion.62 = f32[8,4,64]{2,1,0:T(4,128)S(1)} fusion(bf16[8,128,4,32]{1,3,2,0:T(8,128)(2,1)S(1)} %get-tuple-element.256, f32[4,64,128]{2,1,0:T(8,128)S(1)} %copy.67, pred[8,128]{1,0:T(8,128)(4,1)S(1)} %fusion.61, bf16[8,64,4,32]{1,0,3,2:T(8,128)(2,1)S(1)} %constant_dynamic-slice_fusion.5), kind=kOutput, calls=%fused_computation.41.clone.1 | convolution fusion | flops 18088064 | bytes 533504 | tf_op jit(solution)/shard_map/while/body/eval_jaxpr/sub | solution.py:61
  39.1 3.6 %fusion.64 = f32[8,4,64,32]{2,3,1,0:T(8,128)S(1)} fusion(bf16[8,128,4,32]{1,3,2,0:T(8,128)(2,1)S(1)} %get-tuple-element.258, f32[8,4,64]{2,1,0:T(4,128)S(1)} %fusion.62, f32[8,4,64,128]{3,2,1,0:T(8,128)S(1)} %fusion.63), kind=kOutput, calls=%fused_computation.9.clone.1 | convolution fusion | flops 17565824 | bytes 1581056 | tf_op jit(solution)/shard_map/while/body/eval_jaxpr/rhjk,rkhd->rjhd/dot_general | solution.py:63
  42.7 0.2 copy.68
  42.9 0.1 multiply_convert_fusion.2
  43.0 0.2 convolution_convert_fusion.3
  43.2 0.2 copy.44
  43.4 12.6 %all_to_all.18 = bf16[8,128,128]{2,0,1:T(8,128)(2,1)S(1)} all-to-all(bf16[8,128,128]{2,0,1:T(8,128)(2,1)S(1)} %copy.44), channel_id=1, replica_groups=mesh['grp'=2,'row'=16] {'row'}, dimensions={1} | all-to-all | bytes 524288 | tf_op jit(solution)/shard_map/all_to_all | solution.py:73
  56.0 0.8 %copy.46 = bf16[16,8,8,128]{3,2,1,0:T(8,128)(2,1)} copy(bf16[16,8,8,128]{3,1,2,0:T(8,128)(2,1)S(1)} %bitcast.76) | data formatting | bytes 524288 | tf_op jit(solution)/shard_map/all_to_all | solution.py:73
  (32 shorter events, 0.4 us)
Async XLA Ops:
  0.0 5.2 %copy-start = (bf16[128,4]{0,1:T(4,128)(2,1)S(1)}, bf16[128,4]{0,1:T(4,128)(2,1)}, u32[]{:S(2)}) copy-start(bf16[128,4]{0,1:T(4,128)(2,1)} %param.18) | copy-start | bytes 3076
  0.0 3.8 %copy-start.5 = (bf16[128,128]{1,0:T(8,128)(2,1)S(1)}, bf16[128,128]{1,0:T(8,128)(2,1)}, u32[]{:S(2)}) copy-start(bf16[128,128]{1,0:T(8,128)(2,1)} %param.14) | copy-start | bytes 98308
  0.0 3.8 %copy-start.4 = (bf16[128,128]{1,0:T(8,128)(2,1)S(1)}, bf16[128,128]{1,0:T(8,128)(2,1)}, u32[]{:S(2)}) copy-start(bf16[128,128]{1,0:T(8,128)(2,1)} %param.15) | copy-start | bytes 98308
  0.0 3.8 %copy-start.3 = (bf16[128,128]{1,0:T(8,128)(2,1)S(1)}, bf16[128,128]{1,0:T(8,128)(2,1)}, u32[]{:S(2)}) copy-start(bf16[128,128]{1,0:T(8,128)(2,1)} %param.16) | copy-start | bytes 98308
  0.0 3.8 %copy-start.2 = (bf16[128,128]{1,0:T(8,128)(2,1)S(1)}, bf16[128,128]{1,0:T(8,128)(2,1)}, u32[]{:S(2)}) copy-start(bf16[128,128]{1,0:T(8,128)(2,1)} %param.17) | copy-start | bytes 98308
  4.9 24.3 %copy-start.6 = (s32[8]{0:T(128)S(1)}, s32[8]{0:T(128)}, u32[]{:S(2)}) copy-start(s32[8]{0:T(128)} %param.20) | copy-start | bytes 100
  4.9 24.3 %copy-start.7 = (s32[8]{0:T(128)S(1)}, s32[8]{0:T(128)}, u32[]{:S(2)}) copy-start(s32[8]{0:T(128)} %param.21) | copy-start | bytes 100
  5.0 24.3 %copy-start.1 = (bf16[128,128]{1,0:T(8,128)(2,1)S(1)}, bf16[128,128]{1,0:T(8,128)(2,1)}, u32[]{:S(2)}) copy-start(bf16[128,128]{1,0:T(8,128)(2,1)} %param.19) | copy-start | bytes 98308
where the time goes:
time: 57 us; the launch traced here: 56.8 us
  blocking collectives  36.4 us (64%)
  matrix products  10.6 us (19%)
  other arithmetic  4.09 us (7%)
  local copies, waits for them, and re-layouts  3.88 us (7%)
  loops' own time  1.56 us (3%)
    all_gather x1, blocking collectives, local(): all_bias = lax.all_gather(local_bias, 'row', axis=1, tiled=True)  23.8 us
    all_to_all x1, blocking collectives, local(): lax.all_to_all(result, 'row', split_axis=1, concat_axis=0, tiled=True)  12.6 us
    dot_general x2, matrix products, one_block(): jnp.einsum('rhjk,rkhd->rjhd', weights, value, preferred_element_type=jnp....  7.26 us
    sub x2, matrix products, one_block(): raised = jnp.exp(scores - top)  1.69 us
    another operation x1, loops' own time, local(): blocks = lax.map(one_block, jnp.arange(length // block, dtype=jnp.int32))  1.56 us
    dynamic_slice x2, local copies, waits for them, and re-layouts, local(): blocks = lax.map(one_block, jnp.arange(length // block, dtype=jnp.int32))  1.33 us
    reduce_sum x1, other arithmetic, normalize(): spread = jnp.mean((values - center) ** 2, axis=-1, keepdims=True)  1.32 us
    convert_element_type x1, other arithmetic, normalize(): ((values - center) * lax.rsqrt(spread + 1e-05) * norm_gain).astype(jnp.bf...  1.29 us

commit v1 on v0

--- a/solution.py
+++ b/solution.py
@@ -42,7 +42,12 @@
         positions[None, :] < (window_start + key_length)[:, None]
     )
     factor = 1.0 / head_size**0.5
-    all_bias = lax.all_gather(local_bias, "row", axis=1, tiled=True)
+    ring = [local_bias]
+    for hop in range(15):
+        ring.append(lax.ppermute(ring[-1], "row", [(dev, (dev + 1) % 16) for dev in range(16)]))
+    all_bias = jnp.roll(
+        jnp.concatenate(ring[::-1], axis=1), (lax.axis_index("row") + 1) * ring[0].shape[1], axis=1
+    )
     length = all_bias.shape[1]
     block = math.gcd(length, 64)
 

time: 57 us -> 121 us (2.12)
  waiting for transfers between devices: 0 us -> 86.7 us
  blocking collectives: 36.4 us -> 12.6 us
    ppermute x0 -> x15, waiting for transfers between devices: none -> 86.7 us  [local(): lax.ppermute(ring[-1], 'row', [(dev, (dev + 1) % 16) for dev in range(16)])]
    all_gather x1 -> x0, blocking collectives: 23.8 us -> none  [local(): all_bias = lax.all_gather(local_bias, 'row', axis=1, tiled=True)]
  transfers between devices with their start and end apart: 0 -> 15, of which waited for: 0 -> 15; matrix products, arithmetic and copies ran while one was open for 0% -> 1% of each run, Pallas kernels for 0% -> 0%
where the time goes in v1:
time: 121 us
  waiting for transfers between devices  86.7 us (72%)
  blocking collectives  12.6 us (10%)
  matrix products  10.6 us (9%)
  local copies, waits for them, and re-layouts  4.41 us (4%)
  other arithmetic  4.09 us (3%)
  loops' own time  1.45 us (1%)
    ppermute x15, waiting for transfers between devices, local(): lax.ppermute(ring[-1], 'row', [(dev, (dev + 1) % 16) for dev in range(16)])  86.7 us
    all_to_all x1, blocking collectives, local(): lax.all_to_all(result, 'row', split_axis=1, concat_axis=0, tiled=True)  12.6 us
    dot_general x2, matrix products, one_block(): jnp.einsum('rhjk,rkhd->rjhd', weights, value, preferred_element_type=jnp....  7.26 us
  transfers between devices with their start and end apart: 15, of which 15 were waited for; matrix products, arithmetic and copies ran while one was open for 1% of the time, Pallas kernels for 0%

profile of v1, /device:TPU:0, one launch (start us, length us, event | category | flops | bytes accessed | tf_op | source)
XLA Modules:
  0.0 120.7 jit_solution(8242977535515801586)
XLA Ops:
  0.0 1.1 convert_reduce_fusion
  1.2 1.3 %fusion.17 = f32[8,128]{1,0:T(8,128)S(1)} fusion(bf16[8,128,128]{2,1,0:T(8,128)(2,1)} %param.12, f32[8,128]{1,0:T(8,128)S(1)} %broadcast_multiply_fusion), kind=kLoop, calls=%fused_computation.27 | loop fusion | flops 523264 | bytes 270336 | tf_op jit(solution)/shard_map/reduce_sum | solution.py:13
  2.5 1.3 %fusion.19 = bf16[8,128,128]{2,1,0:T(8,128)(2,1)S(1)} fusion(bf16[8,128,128]{2,1,0:T(8,128)(2,1)} %param.12, f32[128]{0:T(128)} %param.13, f32[8,128]{1,0:T(8,128)S(1)} %add_rsqrt_fusion, f32[8,128]{1,0:T(8,128)S(1)} %broadcast_multiply_fusion), kind=kLoop, calls=%fused_computation.29 | loop fusion | flops 655360 | bytes 532992 | tf_op jit(solution)/shard_map/convert_element_type | solution.py:14
  4.0 0.5 collective-permute-start
  4.5 6.4 %collective-permute-done = f32[4,8,128]{2,0,1:T(4,128)S(1)} collective-permute-done((f32[4,8,128]{2,0,1:T(4,128)S(1)}, f32[4,8,128]{2,0,1:T(4,128)S(1)}, u32[]{:S(2)}, u32[]{:S(2)}) %collective-permute-start) | collective-permute-done | bytes 16416 | tf_op jit(solution)/shard_map/ppermute | solution.py:47
  10.9 5.9 %collective-permute-done.1 = f32[4,8,128]{2,0,1:T(4,128)S(1)} collective-permute-done((f32[4,8,128]{2,0,1:T(4,128)S(1)}, f32[4,8,128]{2,0,1:T(4,128)S(1)}, u32[]{:S(2)}, u32[]{:S(2)}) %collective-permute-start.1) | collective-permute-done | bytes 16416 | tf_op jit(solution)/shard_map/ppermute | solution.py:47
  16.8 5.9 %collective-permute-done.2 = f32[4,8,128]{2,0,1:T(4,128)S(1)} collective-permute-done((f32[4,8,128]{2,0,1:T(4,128)S(1)}, f32[4,8,128]{2,0,1:T(4,128)S(1)}, u32[]{:S(2)}, u32[]{:S(2)}) %collective-permute-start.2) | collective-permute-done | bytes 16416 | tf_op jit(solution)/shard_map/ppermute | solution.py:47
  22.6 5.9 %collective-permute-done.3 = f32[4,8,128]{2,0,1:T(4,128)S(1)} collective-permute-done((f32[4,8,128]{2,0,1:T(4,128)S(1)}, f32[4,8,128]{2,0,1:T(4,128)S(1)}, u32[]{:S(2)}, u32[]{:S(2)}) %collective-permute-start.3) | collective-permute-done | bytes 16416 | tf_op jit(solution)/shard_map/ppermute | solution.py:47
  28.5 5.9 %collective-permute-done.4 = f32[4,8,128]{2,0,1:T(4,128)S(1)} collective-permute-done((f32[4,8,128]{2,0,1:T(4,128)S(1)}, f32[4,8,128]{2,0,1:T(4,128)S(1)}, u32[]{:S(2)}, u32[]{:S(2)}) %collective-permute-start.4) | collective-permute-done | bytes 16416 | tf_op jit(solution)/shard_map/ppermute | solution.py:47
  34.4 5.9 %collective-permute-done.5 = f32[4,8,128]{2,0,1:T(4,128)S(1)} collective-permute-done((f32[4,8,128]{2,0,1:T(4,128)S(1)}, f32[4,8,128]{2,0,1:T(4,128)S(1)}, u32[]{:S(2)}, u32[]{:S(2)}) %collective-permute-start.5) | collective-permute-done | bytes 16416 | tf_op jit(solution)/shard_map/ppermute | solution.py:47
  40.2 5.9 %collective-permute-done.6 = f32[4,8,128]{2,0,1:T(4,128)S(1)} collective-permute-done((f32[4,8,128]{2,0,1:T(4,128)S(1)}, f32[4,8,128]{2,0,1:T(4,128)S(1)}, u32[]{:S(2)}, u32[]{:S(2)}) %collective-permute-start.6) | collective-permute-done | bytes 16416 | tf_op jit(solution)/shard_map/ppermute | solution.py:47
  46.1 5.9 %collective-permute-done.7 = f32[4,8,128]{2,0,1:T(4,128)S(1)} collective-permute-done((f32[4,8,128]{2,0,1:T(4,128)S(1)}, f32[4,8,128]{2,0,1:T(4,128)S(1)}, u32[]{:S(2)}, u32[]{:S(2)}) %collective-permute-start.7) | collective-permute-done | bytes 16416 | tf_op jit(solution)/shard_map/ppermute | solution.py:47
  51.9 5.9 %collective-permute-done.8 = f32[4,8,128]{2,0,1:T(4,128)S(1)} collective-permute-done((f32[4,8,128]{2,0,1:T(4,128)S(1)}, f32[4,8,128]{2,0,1:T(4,128)S(1)}, u32[]{:S(2)}, u32[]{:S(2)}) %collective-permute-start.8) | collective-permute-done | bytes 16416 | tf_op jit(solution)/shard_map/ppermute | solution.py:47
  57.8 5.9 %collective-permute-done.9 = f32[4,8,128]{2,0,1:T(4,128)S(1)} collective-permute-done((f32[4,8,128]{2,0,1:T(4,128)S(1)}, f32[4,8,128]{2,0,1:T(4,128)S(1)}, u32[]{:S(2)}, u32[]{:S(2)}) %collective-permute-start.9) | collective-permute-done | bytes 16416 | tf_op jit(solution)/shard_map/ppermute | solution.py:47
  63.7 5.9 %collective-permute-done.10 = f32[4,8,128]{2,0,1:T(4,128)S(1)} collective-permute-done((f32[4,8,128]{2,0,1:T(4,128)S(1)}, f32[4,8,128]{2,0,1:T(4,128)S(1)}, u32[]{:S(2)}, u32[]{:S(2)}) %collective-permute-start.10) | collective-permute-done | bytes 16416 | tf_op jit(solution)/shard_map/ppermute | solution.py:47
  69.5 5.9 %collective-permute-done.11 = f32[4,8,128]{2,0,1:T(4,128)S(1)} collective-permute-done((f32[4,8,128]{2,0,1:T(4,128)S(1)}, f32[4,8,128]{2,0,1:T(4,128)S(1)}, u32[]{:S(2)}, u32[]{:S(2)}) %collective-permute-start.11) | collective-permute-done | bytes 16416 | tf_op jit(solution)/shard_map/ppermute | solution.py:47
  75.4 5.9 %collective-permute-done.12 = f32[4,8,128]{2,0,1:T(4,128)S(1)} collective-permute-done((f32[4,8,128]{2,0,1:T(4,128)S(1)}, f32[4,8,128]{2,0,1:T(4,128)S(1)}, u32[]{:S(2)}, u32[]{:S(2)}) %collective-permute-start.12) | collective-permute-done | bytes 16416 | tf_op jit(solution)/shard_map/ppermute | solution.py:47
  81.3 0.4 convolution_convert_fusion.1
  81.7 5.4 %collective-permute-done.13 = f32[4,8,128]{2,0,1:T(4,128)S(1)} collective-permute-done((f32[4,8,128]{2,0,1:T(4,128)S(1)}, f32[4,8,128]{2,0,1:T(4,128)S(1)}, u32[]{:S(2)}, u32[]{:S(2)}) %collective-permute-start.13) | collective-permute-done | bytes 16416 | tf_op jit(solution)/shard_map/ppermute | solution.py:47
  88.1 0.3 copy-done.6
  88.4 4.6 %collective-permute-done.14 = f32[4,8,128]{2,0,1:T(4,128)S(1)} collective-permute-done((f32[4,8,128]{2,0,1:T(4,128)S(1)}, f32[4,8,128]{2,0,1:T(4,128)S(1)}, u32[]{:S(2)}, u32[]{:S(2)}) %collective-permute-start.14) | collective-permute-done | bytes 16416 | tf_op jit(solution)/shard_map/ppermute | solution.py:47
  93.4 13.7 %while.11 = (s32[]{:T(128)}, bf16[2,8,64,128]{3,2,0,1:T(8,128)(2,1)S(1)}, s32[2]{0:T(128)S(1)}, bf16[8,128,128]{2,1,0:T(8,128)(2,1)S(1)}, bf16[8,128,4,32]{1,0,3...) while((s32[]{:T(128)}, ...), condition=%wide.region_5.6_spmd.clone, body=%wide.region_2.5_spmd.clone.sunk | while | flops 70456576 | bytes 6081815 | solution.py:76
  93.4 0.6 dynamic_slice.33
  95.0 0.3 fusion.63
  95.3 0.8 fusion.62
  96.2 3.6 %fusion.64 = f32[8,4,64,32]{2,3,1,0:T(8,128)S(1)} fusion(bf16[8,128,4,32]{1,3,2,0:T(8,128)(2,1)S(1)} %get-tuple-element.258, f32[8,4,64]{2,1,0:T(4,128)S(1)} %fusion.62, f32[8,4,64,128]{3,2,1,0:T(8,128)S(1)} %fusion.63), kind=kOutput, calls=%fused_computation.9.clone.1 | convolution fusion | flops 17565824 | bytes 1581056 | tf_op jit(solution)/shard_map/while/body/eval_jaxpr/rhjk,rkhd->rjhd/dot_general | solution.py:68
  100.3 0.6 dynamic_slice.33
  101.8 0.3 fusion.63
  102.2 0.8 fusion.62
  103.0 3.6 %fusion.64 = f32[8,4,64,32]{2,3,1,0:T(8,128)S(1)} fusion(bf16[8,128,4,32]{1,3,2,0:T(8,128)(2,1)S(1)} %get-tuple-element.258, f32[8,4,64]{2,1,0:T(4,128)S(1)} %fusion.62, f32[8,4,64,128]{3,2,1,0:T(8,128)S(1)} %fusion.63), kind=kOutput, calls=%fused_computation.9.clone.1 | convolution fusion | flops 17565824 | bytes 1581056 | tf_op jit(solution)/shard_map/while/body/eval_jaxpr/rhjk,rkhd->rjhd/dot_general | solution.py:68
  107.3 12.6 %all_to_all.18 = bf16[8,128,128]{2,0,1:T(8,128)(2,1)S(1)} all-to-all(bf16[8,128,128]{2,0,1:T(8,128)(2,1)S(1)} %copy.44), channel_id=1, replica_groups=mesh['grp'=2,'row'=16] {'row'}, dimensions={1} | all-to-all | bytes 524288 | tf_op jit(solution)/shard_map/all_to_all | solution.py:78
  120.0 0.8 copy.46
  (94 shorter events, 3.0 us)
Async XLA Ops:
  0.0 3.8 %copy-start = (bf16[128,4]{0,1:T(4,128)(2,1)S(1)}, bf16[128,4]{0,1:T(4,128)(2,1)}, u32[]{:S(2)}) copy-start(bf16[128,4]{0,1:T(4,128)(2,1)} %param.18) | copy-start | bytes 3076
  0.0 81.3 %copy-start.5 = (bf16[128,128]{1,0:T(8,128)(2,1)S(1)}, bf16[128,128]{1,0:T(8,128)(2,1)}, u32[]{:S(2)}) copy-start(bf16[128,128]{1,0:T(8,128)(2,1)} %param.14) | copy-start | bytes 98308
  0.0 81.3 %copy-start.4 = (bf16[128,128]{1,0:T(8,128)(2,1)S(1)}, bf16[128,128]{1,0:T(8,128)(2,1)}, u32[]{:S(2)}) copy-start(bf16[128,128]{1,0:T(8,128)(2,1)} %param.15) | copy-start | bytes 98308
  0.0 81.3 %copy-start.3 = (bf16[128,128]{1,0:T(8,128)(2,1)S(1)}, bf16[128,128]{1,0:T(8,128)(2,1)}, u32[]{:S(2)}) copy-start(bf16[128,128]{1,0:T(8,128)(2,1)} %param.16) | copy-start | bytes 98308
  0.0 81.3 %copy-start.2 = (bf16[128,128]{1,0:T(8,128)(2,1)S(1)}, bf16[128,128]{1,0:T(8,128)(2,1)}, u32[]{:S(2)}) copy-start(bf16[128,128]{1,0:T(8,128)(2,1)} %param.17) | copy-start | bytes 98308
  4.0 6.9 %collective-permute-start = (f32[4,8,128]{2,0,1:T(4,128)S(1)}, f32[4,8,128]{2,0,1:T(4,128)S(1)}, u32[]{:S(2)}, u32[]{:S(2)}) collective-permute-start(f32[4,8,128]{2,0,1:T(4,128)S(1)} %convolution_bitcast_fusion), channel_id=1, source_target_pairs={{0,1},{1,2},{2,3},{3,4},{4,5},{5,6},{6,7},{7,8},{8,9},{9,10},{10,1... | collective-permute-start | bytes 49160 | tf_op jit(solution)/shard_map/ppermute | solution.py:47
  10.9 5.9 %collective-permute-start.1 = (f32[4,8,128]{2,0,1:T(4,128)S(1)}, f32[4,8,128]{2,0,1:T(4,128)S(1)}, u32[]{:S(2)}, u32[]{:S(2)}) collective-permute-start(f32[4,8,128]{2,0,1:T(4,128)S(1)} %collective-permute-done), channel_id=1, source_target_pairs={{0,1},{1,2},{2,3},{3,4},{4,5},{5,6},{6,7},{7,8},{8,9},{9,10},{10,1... | collective-permute-start | bytes 49160 | tf_op jit(solution)/shard_map/ppermute | solution.py:47
  16.8 5.9 %collective-permute-start.2 = (f32[4,8,128]{2,0,1:T(4,128)S(1)}, f32[4,8,128]{2,0,1:T(4,128)S(1)}, u32[]{:S(2)}, u32[]{:S(2)}) collective-permute-start(f32[4,8,128]{2,0,1:T(4,128)S(1)} %collective-permute-done.1), channel_id=1, source_target_pairs={{0,1},{1,2},{2,3},{3,4},{4,5},{5,6},{6,7},{7,8},{8,9},{9,10},{10,1... | collective-permute-start | bytes 49160 | tf_op jit(solution)/shard_map/ppermute | solution.py:47
  22.6 5.9 %collective-permute-start.3 = (f32[4,8,128]{2,0,1:T(4,128)S(1)}, f32[4,8,128]{2,0,1:T(4,128)S(1)}, u32[]{:S(2)}, u32[]{:S(2)}) collective-permute-start(f32[4,8,128]{2,0,1:T(4,128)S(1)} %collective-permute-done.2), channel_id=1, source_target_pairs={{0,1},{1,2},{2,3},{3,4},{4,5},{5,6},{6,7},{7,8},{8,9},{9,10},{10,1... | collective-permute-start | bytes 49160 | tf_op jit(solution)/shard_map/ppermute | solution.py:47
  28.5 5.9 %collective-permute-start.4 = (f32[4,8,128]{2,0,1:T(4,128)S(1)}, f32[4,8,128]{2,0,1:T(4,128)S(1)}, u32[]{:S(2)}, u32[]{:S(2)}) collective-permute-start(f32[4,8,128]{2,0,1:T(4,128)S(1)} %collective-permute-done.3), channel_id=1, source_target_pairs={{0,1},{1,2},{2,3},{3,4},{4,5},{5,6},{6,7},{7,8},{8,9},{9,10},{10,1... | collective-permute-start | bytes 49160 | tf_op jit(solution)/shard_map/ppermute | solution.py:47
  34.4 5.9 %collective-permute-start.5 = (f32[4,8,128]{2,0,1:T(4,128)S(1)}, f32[4,8,128]{2,0,1:T(4,128)S(1)}, u32[]{:S(2)}, u32[]{:S(2)}) collective-permute-start(f32[4,8,128]{2,0,1:T(4,128)S(1)} %collective-permute-done.4), channel_id=1, source_target_pairs={{0,1},{1,2},{2,3},{3,4},{4,5},{5,6},{6,7},{7,8},{8,9},{9,10},{10,1... | collective-permute-start | bytes 49160 | tf_op jit(solution)/shard_map/ppermute | solution.py:47
  40.2 5.9 %collective-permute-start.6 = (f32[4,8,128]{2,0,1:T(4,128)S(1)}, f32[4,8,128]{2,0,1:T(4,128)S(1)}, u32[]{:S(2)}, u32[]{:S(2)}) collective-permute-start(f32[4,8,128]{2,0,1:T(4,128)S(1)} %collective-permute-done.5), channel_id=1, source_target_pairs={{0,1},{1,2},{2,3},{3,4},{4,5},{5,6},{6,7},{7,8},{8,9},{9,10},{10,1... | collective-permute-start | bytes 49160 | tf_op jit(solution)/shard_map/ppermute | solution.py:47
  46.1 5.9 %collective-permute-start.7 = (f32[4,8,128]{2,0,1:T(4,128)S(1)}, f32[4,8,128]{2,0,1:T(4,128)S(1)}, u32[]{:S(2)}, u32[]{:S(2)}) collective-permute-start(f32[4,8,128]{2,0,1:T(4,128)S(1)} %collective-permute-done.6), channel_id=1, source_target_pairs={{0,1},{1,2},{2,3},{3,4},{4,5},{5,6},{6,7},{7,8},{8,9},{9,10},{10,1... | collective-permute-start | bytes 49160 | tf_op jit(solution)/shard_map/ppermute | solution.py:47
  51.9 5.9 %collective-permute-start.8 = (f32[4,8,128]{2,0,1:T(4,128)S(1)}, f32[4,8,128]{2,0,1:T(4,128)S(1)}, u32[]{:S(2)}, u32[]{:S(2)}) collective-permute-start(f32[4,8,128]{2,0,1:T(4,128)S(1)} %collective-permute-done.7), channel_id=1, source_target_pairs={{0,1},{1,2},{2,3},{3,4},{4,5},{5,6},{6,7},{7,8},{8,9},{9,10},{10,1... | collective-permute-start | bytes 49160 | tf_op jit(solution)/shard_map/ppermute | solution.py:47
  57.8 5.9 %collective-permute-start.9 = (f32[4,8,128]{2,0,1:T(4,128)S(1)}, f32[4,8,128]{2,0,1:T(4,128)S(1)}, u32[]{:S(2)}, u32[]{:S(2)}) collective-permute-start(f32[4,8,128]{2,0,1:T(4,128)S(1)} %collective-permute-done.8), channel_id=1, source_target_pairs={{0,1},{1,2},{2,3},{3,4},{4,5},{5,6},{6,7},{7,8},{8,9},{9,10},{10,1... | collective-permute-start | bytes 49160 | tf_op jit(solution)/shard_map/ppermute | solution.py:47
  63.7 5.9 %collective-permute-start.10 = (f32[4,8,128]{2,0,1:T(4,128)S(1)}, f32[4,8,128]{2,0,1:T(4,128)S(1)}, u32[]{:S(2)}, u32[]{:S(2)}) collective-permute-start(f32[4,8,128]{2,0,1:T(4,128)S(1)} %collective-permute-done.9), channel_id=1, source_target_pairs={{0,1},{1,2},{2,3},{3,4},{4,5},{5,6},{6,7},{7,8},{8,9},{9,10},{10,1... | collective-permute-start | bytes 49160 | tf_op jit(solution)/shard_map/ppermute | solution.py:47
  69.5 5.9 %collective-permute-start.11 = (f32[4,8,128]{2,0,1:T(4,128)S(1)}, f32[4,8,128]{2,0,1:T(4,128)S(1)}, u32[]{:S(2)}, u32[]{:S(2)}) collective-permute-start(f32[4,8,128]{2,0,1:T(4,128)S(1)} %collective-permute-done.10), channel_id=1, source_target_pairs={{0,1},{1,2},{2,3},{3,4},{4,5},{5,6},{6,7},{7,8},{8,9},{9,10},{10,1... | collective-permute-start | bytes 49160 | tf_op jit(solution)/shard_map/ppermute | solution.py:47
  75.4 5.9 %collective-permute-start.12 = (f32[4,8,128]{2,0,1:T(4,128)S(1)}, f32[4,8,128]{2,0,1:T(4,128)S(1)}, u32[]{:S(2)}, u32[]{:S(2)}) collective-permute-start(f32[4,8,128]{2,0,1:T(4,128)S(1)} %collective-permute-done.11), channel_id=1, source_target_pairs={{0,1},{1,2},{2,3},{3,4},{4,5},{5,6},{6,7},{7,8},{8,9},{9,10},{10,1... | collective-permute-start | bytes 49160 | tf_op jit(solution)/shard_map/ppermute | solution.py:47
  81.2 5.9 %collective-permute-start.13 = (f32[4,8,128]{2,0,1:T(4,128)S(1)}, f32[4,8,128]{2,0,1:T(4,128)S(1)}, u32[]{:S(2)}, u32[]{:S(2)}) collective-permute-start(f32[4,8,128]{2,0,1:T(4,128)S(1)} %collective-permute-done.12), channel_id=1, source_target_pairs={{0,1},{1,2},{2,3},{3,4},{4,5},{5,6},{6,7},{7,8},{8,9},{9,10},{10,1... | collective-permute-start | bytes 49160 | tf_op jit(solution)/shard_map/ppermute | solution.py:47
  87.1 5.9 %collective-permute-start.14 = (f32[4,8,128]{2,0,1:T(4,128)S(1)}, f32[4,8,128]{2,0,1:T(4,128)S(1)}, u32[]{:S(2)}, u32[]{:S(2)}) collective-permute-start(f32[4,8,128]{2,0,1:T(4,128)S(1)} %collective-permute-done.13), channel_id=1, source_target_pairs={{0,1},{1,2},{2,3},{3,4},{4,5},{5,6},{6,7},{7,8},{8,9},{9,10},{10,1... | collective-permute-start | bytes 49160 | tf_op jit(solution)/shard_map/ppermute | solution.py:47
  87.7 0.7 copy-start.6
  87.8 0.7 copy-start.7
  88.0 5.4 %copy-start.1 = (bf16[128,128]{1,0:T(8,128)(2,1)S(1)}, bf16[128,128]{1,0:T(8,128)(2,1)}, u32[]{:S(2)}) copy-start(bf16[128,128]{1,0:T(8,128)(2,1)} %param.19) | copy-start | bytes 98308
